TPU v7x, 32 devices: a whole 2x2x4 slice. The times are simulated.
32 devices in a mesh: groups: 2 (over x), canvas: 16 (over z, y, core).
Axes of the slice: x: 2, y: 2, z: 4, core: 2. Of those that a mesh axis runs over, the one named last changes fastest.
Arguments:
- net_slabs: int32 [65536, 2], P(('groups', 'canvas')), parts along dimension 0, may hold values from 0 to 15, all different within a row; in each aligned block of 2048 rows (0 to 2047, 2048 to 4095, ...) at most 512 rows name the same one
- row_offsets: int32 [65536, 2], P(('groups', 'canvas')), parts along dimension 0, may hold values from 0 to 15
- left_column: int32 [65536], P(('groups', 'canvas')), parts along dimension 0, may hold values from 0 to 8191
- column_span: int32 [65536], P(('groups', 'canvas')), parts along dimension 0, may hold values from 1 to 16
- pin_counts: int32 [65536], P(('groups', 'canvas')), parts along dimension 0, may hold values from 2 to 64
- tile_features: bfloat16 [7, 512, 8192], P(None, ('groups', 'canvas')), parts along dimension 1, may hold values from -6 to 6
- cotangent: float32 [512, 8192], P(('groups', 'canvas')), parts along dimension 0, may hold values from -0.0124296114 to 0.0124296114
- first_weight: bfloat16 [64, 8], replicated, may hold values from -2 to 2
- first_bias: float32 [64], replicated, may hold values from -3 to 3
- second_weight: bfloat16 [64, 64], replicated, may hold values from -0.75 to 0.75
- second_bias: float32 [64], replicated, may hold values from -3 to 3
- readout_weight: bfloat16 [64], replicated, may hold values from -0.75 to 0.75
- readout_bias: float32 [1], replicated, may hold values from -3 to 3
Outputs:
- prediction: float32 [512, 8192], P(('groups', 'canvas')), parts along dimension 0
- grad_first: float32 [128, 8], P('groups'), parts along dimension 0
- grad_first_bias: float32 [128], P('groups'), parts along dimension 0
- grad_second: float32 [128, 64], P('groups'), parts along dimension 0
- grad_second_bias: float32 [128], P('groups'), parts along dimension 0
- grad_readout: float32 [128], P('groups'), parts along dimension 0
- grad_readout_bias: float32 [2], P('groups'), parts along dimension 0
There are 2 independent parts, one for each index of `groups`. A program takes and returns all parts, laid end to end along the dimension named above; an argument that names none is the same for every part. Nothing has to cross between parts.
Inputs may be any that keep to these rules, and one draw needn't show every extreme that they name: `net_slabs`: the two slab numbers of a net differ. Among the 2048 rows of one device no slab number is named by more than 512 rows, and in some device's rows one slab number is named by exactly 512 rows.
All inputs are finite; a program needn't handle non-finite values.
Results may differ from a plain program's by a relative error of at most 0.0071.
Values sent between devices are 32-bit elements; how exact they have to be, the bound alone decides.
A program may use at most 64 MiB of HBM per device.

v0:
```python
import jax
import jax.numpy as jnp
from jax import lax
from jax.sharding import PartitionSpec as P

root_half = 0.7071067811865476
inv_root_tau = 0.3989422804014327


def gelu_value(value):
    return 0.5 * value * (1.0 + jax.scipy.special.erf(value * root_half))


def gelu_slope(value):
    return (
        0.5 * (1.0 + jax.scipy.special.erf(value * root_half))
        + value * jnp.exp(-0.5 * value * value) * inv_root_tau
    )


def cell_block(
    inputs,
    grad_row,
    first_weight,
    first_bias,
    second_weight,
    second_bias,
    readout_weight,
    readout_bias,
):
    first_pre = (
        jnp.dot(first_weight, inputs, preferred_element_type=jnp.float32) + first_bias[:, None]
    )
    act_one = gelu_value(first_pre).astype(jnp.bfloat16)
    second_pre = (
        jnp.dot(second_weight, act_one, preferred_element_type=jnp.float32) + second_bias[:, None]
    )
    act_two = gelu_value(second_pre).astype(jnp.bfloat16)
    prediction = (
        jnp.dot(readout_weight[None, :], act_two, preferred_element_type=jnp.float32)[0]
        + readout_bias[0]
    )
    grad_readout = jnp.sum(act_two.astype(jnp.float32) * grad_row[None, :], axis=1)
    grad_readout_bias = jnp.sum(grad_row).reshape(1)
    delta_two_full = (
        readout_weight.astype(jnp.float32)[:, None] * grad_row[None, :] * gelu_slope(second_pre)
    )
    delta_two = delta_two_full.astype(jnp.bfloat16)
    grad_second = jnp.dot(delta_two, act_one.T, preferred_element_type=jnp.float32)
    grad_second_bias = jnp.sum(delta_two_full, axis=1)
    back_one = jnp.dot(second_weight.T, delta_two, preferred_element_type=jnp.float32)
    delta_one_full = back_one * gelu_slope(first_pre)
    delta_one = delta_one_full.astype(jnp.bfloat16)
    grad_first = jnp.dot(delta_one, inputs.T, preferred_element_type=jnp.float32)
    grad_first_bias = jnp.sum(delta_one_full, axis=1)
    return (
        prediction,
        (
            grad_first,
            grad_first_bias,
            grad_second,
            grad_second_bias,
            grad_readout,
            grad_readout_bias,
        ),
    )


def per_device(
    net_slabs,
    row_offsets,
    left_column,
    column_span,
    pin_counts,
    tile_features,
    cotangent,
    first_weight,
    first_bias,
    second_weight,
    second_bias,
    readout_weight,
    readout_bias,
):
    devices = lax.axis_size("canvas")
    slab_rows = tile_features.shape[1]
    canvas_width = tile_features.shape[2]
    nets_here = pin_counts.shape[0]
    capacity = 4 * nets_here // devices
    highest = lax.Precision.HIGHEST
    first_is_low = net_slabs[:, 0] <= net_slabs[:, 1]
    low_slab = jnp.minimum(net_slabs[:, 0], net_slabs[:, 1])
    high_slab = jnp.maximum(net_slabs[:, 0], net_slabs[:, 1])
    low_offset = jnp.where(first_is_low, row_offsets[:, 0], row_offsets[:, 1])
    high_offset = jnp.where(first_is_low, row_offsets[:, 1], row_offsets[:, 0])
    right_edge = jnp.minimum(left_column + column_span, canvas_width)
    span_columns = (right_edge - left_column).astype(jnp.float32)
    span_rows = ((high_slab - low_slab) * slab_rows + high_offset - low_offset).astype(jnp.float32)
    net_weight = (
        jnp.sqrt(pin_counts.astype(jnp.float32))
        * (span_columns + span_rows)
        / (span_columns * span_rows)
    )
    target_slab = jnp.concatenate([low_slab, high_slab])
    local_row = jnp.concatenate([low_offset, high_offset])
    start_column = jnp.concatenate([left_column, left_column])
    end_column = jnp.concatenate([right_edge, right_edge])
    amounts = jnp.concatenate([net_weight, -net_weight])
    item_count = target_slab.shape[0]
    slab_ids = jnp.arange(devices, dtype=jnp.int32)
    slab_hot = (target_slab[:, None] == slab_ids[None, :]).astype(jnp.bfloat16)
    block_len = 128
    block_count = item_count // block_len
    blocked_hot = slab_hot.reshape(block_count, block_len, devices)
    lower_ones = (jnp.arange(block_len)[:, None] >= jnp.arange(block_len)[None, :]).astype(
        jnp.bfloat16
    )
    inclusive = jnp.einsum(
        "ij,bjd->bid", lower_ones, blocked_hot, preferred_element_type=jnp.float32
    )
    block_totals = inclusive[:, -1, :]
    block_start = jnp.cumsum(block_totals, axis=0) - block_totals
    counted = (inclusive + block_start[:, None, :] - 1.0) * blocked_hot.astype(jnp.float32)
    slot_rank = jnp.sum(counted, axis=2).reshape(item_count).astype(jnp.int32)
    payload = jnp.stack(
        [
            amounts,
            (local_row * canvas_width + start_column).astype(jnp.float32),
            end_column.astype(jnp.float32),
        ]
    )
    dest_mask = (slab_ids[:, None] == target_slab[None, :]).astype(jnp.float32)
    left_side = (payload[:, None, :] * dest_mask[None, :, :]).reshape(3 * devices, item_count)
    rank_hot = (slot_rank[:, None] == jnp.arange(capacity, dtype=jnp.int32)[None, :]).astype(
        jnp.float32
    )
    send_items = jnp.dot(
        left_side, rank_hot, precision=highest, preferred_element_type=jnp.float32
    ).reshape(3, devices, capacity)
    got_items = lax.all_to_all(send_items, "canvas", split_axis=1, concat_axis=1, tiled=True)
    got_items = got_items.reshape(3, -1)
    got_values = got_items[0]
    got_place = got_items[1].astype(jnp.int32)
    got_end = got_items[2].astype(jnp.int32)
    got_row = got_place // canvas_width
    end_place = jnp.where(got_end < canvas_width, got_row * canvas_width + got_end, 0)
    end_values = jnp.where(got_end < canvas_width, -got_values, 0.0)
    event_place = jnp.concatenate([got_place, end_place])
    event_values = jnp.concatenate([got_values, end_values])
    lane_width = 256
    lane_groups = slab_rows * canvas_width // lane_width
    coarse_hot = (
        (event_place // lane_width)[:, None] == jnp.arange(lane_groups, dtype=jnp.int32)[None, :]
    ).astype(jnp.float32)
    fine_hot = (
        (event_place % lane_width)[:, None] == jnp.arange(lane_width, dtype=jnp.int32)[None, :]
    ).astype(jnp.float32) * event_values[:, None]
    edges = lax.dot_general(
        coarse_hot,
        fine_hot,
        (((0,), (0,)), ((), ())),
        precision=highest,
        preferred_element_type=jnp.float32,
    )
    upper_ones = (jnp.arange(lane_width)[:, None] <= jnp.arange(lane_width)[None, :]).astype(
        jnp.float32
    )
    inner = jnp.dot(edges, upper_ones, precision=highest, preferred_element_type=jnp.float32)
    inner = inner.reshape(slab_rows, canvas_width // lane_width, lane_width)
    group_totals = inner[:, :, -1]
    group_before = jnp.cumsum(group_totals, axis=1) - group_totals
    across = (inner + group_before[:, :, None]).reshape(slab_rows, canvas_width)
    column_block = lax.all_to_all(across, "canvas", split_axis=1, concat_axis=0, tiled=True)
    columns_done = jnp.cumsum(column_block, axis=0)
    demand = lax.all_to_all(columns_done, "canvas", split_axis=0, concat_axis=1, tiled=True)
    level = jnp.log1p(demand).astype(jnp.bfloat16)

    def row_step(totals, row_index):
        inputs = jnp.concatenate(
            [level[row_index][None, :], tile_features[:, row_index, :]], axis=0
        )
        prediction, grads = cell_block(
            inputs,
            cotangent[row_index],
            first_weight,
            first_bias,
            second_weight,
            second_bias,
            readout_weight,
            readout_bias,
        )
        return (tuple((a + b for a, b in zip(totals, grads))), prediction)

    hidden_units = first_weight.shape[0]
    in_channels = first_weight.shape[1]
    start = (
        jnp.zeros((hidden_units, in_channels), jnp.float32),
        jnp.zeros((hidden_units,), jnp.float32),
        jnp.zeros((hidden_units, hidden_units), jnp.float32),
        jnp.zeros((hidden_units,), jnp.float32),
        jnp.zeros((hidden_units,), jnp.float32),
        jnp.zeros((1,), jnp.float32),
    )
    totals, prediction = lax.scan(row_step, start, jnp.arange(slab_rows, dtype=jnp.int32))
    summed = lax.psum((totals[0], totals[1], totals[2], totals[3], totals[4], totals[5]), "canvas")
    return (prediction, summed[0], summed[1], summed[2], summed[3], summed[4], summed[5])


def solution(mesh):
    in_specs = (
        P(("groups", "canvas"), None),
        P(("groups", "canvas"), None),
        P(("groups", "canvas")),
        P(("groups", "canvas")),
        P(("groups", "canvas")),
        P(None, ("groups", "canvas"), None),
        P(("groups", "canvas"), None),
        P(),
        P(),
        P(),
        P(),
        P(),
        P(),
    )
    out_specs = (
        P(("groups", "canvas"), None),
        P("groups", None),
        P("groups"),
        P("groups", None),
        P("groups"),
        P("groups"),
        P("groups"),
    )
    return jax.shard_map(
        per_device, mesh=mesh, in_specs=in_specs, out_specs=out_specs, check_vma=False
    )
```

profile of v0, /device:TPU:0, one launch (start us, length us, event | category | flops | bytes accessed | tf_op | source)
XLA Modules:
  0.0 400.1 jit_solution(13370060249048675453)
XLA Ops:
  4.0 3.2 fusion.29
  7.3 15.1 %all_to_all.34 = f32[3,16,512]{2,0,1:T(4,128)S(1)} all-to-all(f32[3,16,512]{2,0,1:T(4,128)S(1)} %copy.90), channel_id=1, replica_groups=mesh['groups'=2,'canvas'=16] {'canvas'}, dimensions={1} | all-to-all | bytes 196608 | tf_op jit(solution)/shard_map/all_to_all | solution.py:139
  22.7 4.6 %fusion.75 = f32[16384,256]{1,0:T(8,128)S(1)} fusion(f32[16384]{0:T(1024)S(1)} %pad_maximum_fusion.4, s32[16384]{0:T(1024)S(1)} %get-tuple-element.338), kind=kLoop, calls=%fused_computation.44.clone.2 | loop fusion | flops 8388608 | bytes 16908288 | tf_op jit(solution)/shard_map/dot_general | solution.py:157
  27.3 32.5 %fusion.22 = f32[512,256]{1,0:T(8,128)S(1)} fusion(s32[16384]{0:T(1024)S(1)} %get-tuple-element.339, f32[16384,256]{1,0:T(8,128)S(1)} %fusion.75), kind=kOutput, calls=%fused_computation.43 | convolution fusion | flops 25778192384 | bytes 17367040 | tf_op jit(solution)/shard_map/dot_general | solution.py:157
  61.5 17.1 %all_to_all.35 = f32[16,16,512]{2,0,1:T(8,128)S(1)} all-to-all(f32[16,16,512]{2,0,1:T(8,128)S(1)} %copy.93), channel_id=1, replica_groups=mesh['groups'=2,'canvas'=16] {'canvas'}, dimensions={1} | all-to-all | bytes 1048576 | tf_op jit(solution)/shard_map/all_to_all | solution.py:172
  80.0 4.0 %all-to-all-start.2 = ((f32[16,16,512]{2,1,0:T(8,128)}), f32[16,16,512]{2,1,0:T(8,128)S(1)}, u32[]{:S(2)}, u32[]{:S(2)}) async-start(f32[16,16,512]{2,1,0:T(8,128)} %bitcast.28), calls=%async_computation.2 | async-start | bytes 1048576 | tf_op jit(solution)/shard_map/all_to_all | solution.py:174
  84.2 2.5 copy.97
  86.7 11.8 %all-to-all-done.2 = f32[16,16,512]{2,1,0:T(8,128)S(1)} async-done(((f32[16,16,512]{2,1,0:T(8,128)}), f32[16,16,512]{2,1,0:T(8,128)S(1)}, u32[]{:S(2)}, u32[]{:S(2)}) %all-to-all-start.2) | async-done | bytes 524320 | tf_op jit(solution)/shard_map/all_to_all | solution.py:174
  98.8 239.3 %while.23 = (s32[]{:T(128)}, f32[64,8]{0,1:T(8,128)S(1)}, f32[64]{0:T(128)S(1)}, f32[64,64]{1,0:T(8,128)S(1)}, f32[64]{0:T(128)S(1)}, /*index=5*/f32[64]{0:T(128...) while((s32[]{:T(128)}, f32[64,8]{0,1:T(8,128)S(1)}, ...), condition=%wide.region_10.11_spmd.clone, body=%wide.region_5.10_spmd.clone.sunk | while | flops 238576896 | bytes 40691396 | solution.py:203
  103.9 2.8 multiply_reduce_fusion.3
  111.3 1.8 dynamic_update_slice.6
  118.9 2.8 multiply_reduce_fusion.3
  126.2 1.8 dynamic_update_slice.6
  133.9 2.8 multiply_reduce_fusion.3
  141.2 1.8 dynamic_update_slice.6
  148.8 2.8 multiply_reduce_fusion.3
  156.1 1.8 dynamic_update_slice.6
  163.8 2.8 multiply_reduce_fusion.3
  171.1 1.8 dynamic_update_slice.6
  178.7 2.8 multiply_reduce_fusion.3
  186.0 1.8 dynamic_update_slice.6
  193.7 2.8 multiply_reduce_fusion.3
  208.6 2.8 multiply_reduce_fusion.3
  223.6 2.8 multiply_reduce_fusion.3
  238.6 2.8 multiply_reduce_fusion.3
  253.5 2.8 multiply_reduce_fusion.3
  268.5 2.8 multiply_reduce_fusion.3
  283.4 2.8 multiply_reduce_fusion.3
  298.4 2.8 multiply_reduce_fusion.3
  313.3 2.8 multiply_reduce_fusion.3
  328.3 2.8 multiply_reduce_fusion.3
  338.1 62.0 %all-reduce = (f32[64,8]{0,1:T(8,128)}, f32[64]{0:T(128)}, f32[64,64]{1,0:T(8,128)}, f32[64]{0:T(128)}, f32[64]{0:T(128)}, /*index=5*/f32[1]{0:T(128)}) all-reduce(f32[64,8]{0,1:T(8,128)S(1)} %get-tuple-element.106, f32[64]{0:T(128)S(1)} %get-tuple-element.107, ...), channel_id=1, replica_groups=mesh['groups'=2,'canvas'=16] {'canvas'}, use_global_device_ids=true, to_apply=%region_11.12 | all-reduce | flops 4801 | bytes 38408 | tf_op jit(solution)/shard_map/psum | solution.py:204
  (479 shorter events, 146.0 us)
Async XLA Ops:
  80.0 18.5 %all-to-all-start.2 = ((f32[16,16,512]{2,1,0:T(8,128)}), f32[16,16,512]{2,1,0:T(8,128)S(1)}, u32[]{:S(2)}, u32[]{:S(2)}) async-start(f32[16,16,512]{2,1,0:T(8,128)} %bitcast.28), calls=%async_computation.2 | async-start | bytes 1048576 | tf_op jit(solution)/shard_map/all_to_all | solution.py:174
  84.1 14.6 %copy-start.7 = (bf16[64,8]{0,1:T(8,128)(2,1)S(1)}, bf16[64,8]{0,1:T(8,128)(2,1)}, u32[]{:S(2)}) copy-start(bf16[64,8]{0,1:T(8,128)(2,1)} %param.22) | copy-start | bytes 3076
  84.1 14.6 %copy-start.9 = (bf16[64]{0:T(256)(128)(2,1)S(1)}, bf16[64]{0:T(256)(128)(2,1)}, u32[]{:S(2)}) copy-start(bf16[64]{0:T(256)(128)(2,1)} %param.26) | copy-start | bytes 388
  84.1 14.6 %copy-start.10 = (f32[64]{0:T(128)S(1)}, f32[64]{0:T(128)}, u32[]{:S(2)}) copy-start(f32[64]{0:T(128)} %param.23) | copy-start | bytes 772
  84.1 14.6 %copy-start.12 = (bf16[64,64]{1,0:T(8,128)(2,1)S(1)}, bf16[64,64]{1,0:T(8,128)(2,1)}, u32[]{:S(2)}) copy-start(bf16[64,64]{1,0:T(8,128)(2,1)} %param.24) | copy-start | bytes 24580
  84.2 14.6 %copy-start.13 = (f32[64]{0:T(128)S(1)}, f32[64]{0:T(128)}, u32[]{:S(2)}) copy-start(f32[64]{0:T(128)} %param.25) | copy-start | bytes 772
  109.9 3.8 copy-start.3
  109.9 3.8 copy-start.5
  124.8 3.8 copy-start.3
  124.8 3.8 copy-start.5
  139.8 3.8 copy-start.3
  139.8 3.8 copy-start.5
  154.7 3.8 copy-start.3
  154.8 3.8 copy-start.5
  169.7 3.8 copy-start.3
  169.7 3.8 copy-start.5
  184.7 3.8 copy-start.3
  184.7 3.8 copy-start.5
  199.6 3.8 copy-start.3
  199.6 3.8 copy-start.5
  214.6 3.8 copy-start.3
  214.6 3.8 copy-start.5
  229.5 3.8 copy-start.3
  229.5 3.8 copy-start.5
  244.5 3.8 copy-start.3
  244.5 3.8 copy-start.5
  259.4 3.8 copy-start.3
  259.4 3.8 copy-start.5
  274.4 3.8 copy-start.3
  274.4 3.8 copy-start.5
  289.4 3.8 copy-start.3
  289.4 3.8 copy-start.5
  (73 other events, 175.1 us)
where the time goes:
time: 403 us; the launch traced here: 400 us
  matrix products  153 us (38%)
  blocking collectives  94.2 us (23%)
  local copies, waits for them, and re-layouts  46.6 us (12%)
  other arithmetic  44.9 us (11%)
  loops' own time  44.8 us (11%)
  waiting for transfers between devices  11.8 us (3%)
  starting transfers between devices  4.03 us (1%)
    psum x1, blocking collectives, per_device(): lax.psum((totals[0], totals[1], totals[2], totals[3], totals[4], totals[5...  62 us
    another operation x1, loops' own time, per_device(): lax.scan(row_step, start, jnp.arange(slab_rows, dtype=jnp.int32))  44.8 us
    dot_general x16, matrix products, cell_block(): jnp.dot(second_weight, act_one, preferred_element_type=jnp.float32)  44.7 us
    dot_general x1, matrix products, per_device(): lax.dot_general(coarse_hot, fine_hot, (((0,), (0,)), ((), ())), precision...  32.5 us
    dynamic_update_slice x16, local copies, waits for them, and re-layouts, per_device(): lax.scan(row_step, start, jnp.arange(slab_rows, dtype=jnp.int32))  28.3 us
    dot_general x16, matrix products, cell_block(): jnp.dot(delta_two, act_one.T, preferred_element_type=jnp.float32)  27.9 us
    reduce_sum x16, other arithmetic, cell_block(): grad_readout_bias = jnp.sum(grad_row).reshape(1)  26.1 us
    dot_general x16, matrix products, cell_block(): jnp.dot(second_weight.T, delta_two, preferred_element_type=jnp.float32)  21.5 us
  transfers between devices with their start and end apart: 1, of which 1 were waited for; matrix products, arithmetic and copies ran while one was open for 1% of the time, Pallas kernels for 0%

commit v1 on v0

v1 whole, which is shorter than its diff:
```python
import functools
import jax
import jax.numpy as jnp
from jax import lax
from jax.experimental import pallas as pl
from jax.experimental.pallas import tpu as pltpu
from jax.sharding import PartitionSpec as P

root_half = 0.7071067811865476
inv_root_tau = 0.3989422804014327
log2e = 1.4426950408889634
f32 = jnp.float32
bf16 = jnp.bfloat16
i32 = jnp.int32
NT = (((1,), (1,)), ((), ()))


def iota(shape, dim):
    return lax.broadcasted_iota(i32, shape, dim)


def mlp_body(rows_per, demand_ref, base_ref, feat_ref, cot_ref, w1_ref, b1_ref, w2_ref, b2_ref, ro_ref, rb_ref,
             pred_ref, grads_ref,
             w1x, w2x, w2t, rox, col, acc1, acc2, accr, accb):
    step = pl.program_id(0)
    slab_rows, width = demand_ref.shape
    hidden, cin = w1_ref.shape
    block = rows_per * hidden
    groups = slab_rows // rows_per
    depth = (cin + 1) * slab_rows

    @pl.when(step == 0)
    def _():
        pick = (iota((block, hidden), 0) % hidden == iota((block, hidden), 1)).astype(bf16)
        pick_f = pick.astype(f32)
        spread = (iota((cin, depth), 1) // slab_rows == iota((cin, depth), 0)).astype(bf16)
        tall = jnp.dot(pick, w1_ref[...], preferred_element_type=f32).astype(bf16)
        wide = jnp.dot(tall, spread, preferred_element_type=f32)
        for g in range(groups):
            keep = (iota((block, depth), 0) // hidden + g * rows_per) == iota((block, depth), 1) % slab_rows
            w1x[g] = jnp.where(keep, wide, 0.0).astype(bf16)
        same = iota((block, block), 0) // hidden == iota((block, block), 1) // hidden
        down = jnp.dot(pick, w2_ref[...], preferred_element_type=f32).astype(bf16)
        full = lax.dot_general(down, pick, NT, preferred_element_type=f32)
        w2x[...] = jnp.where(same, full, 0.0).astype(bf16)
        flip = lax.dot_general(pick, w2_ref[...], (((1,), (1,)), ((), ())), preferred_element_type=f32).astype(bf16)
        full_t = lax.dot_general(flip, pick, NT, preferred_element_type=f32)
        w2t[...] = jnp.where(same, full_t, 0.0).astype(bf16)
        ro_wide = lax.dot_general(ro_ref[...], pick, NT, preferred_element_type=f32)
        ro_rows = jnp.broadcast_to(ro_wide, (8, block))
        rox[...] = jnp.where(iota((8, block), 0) == iota((8, block), 1) // hidden, ro_rows, 0.0).astype(bf16)
        col[0] = jnp.broadcast_to(jnp.sum(pick_f * b1_ref[...], axis=1, keepdims=True), (block, 128))
        col[1] = jnp.broadcast_to(jnp.sum(pick_f * b2_ref[...], axis=1, keepdims=True), (block, 128))
        col[2] = jnp.broadcast_to(jnp.sum(pick_f * ro_ref[...].astype(f32), axis=1, keepdims=True), (block, 128))
        acc1[...] = jnp.zeros_like(acc1)
        acc2[...] = jnp.zeros_like(acc2)
        accr[...] = jnp.zeros_like(accr)
        accb[...] = jnp.zeros_like(accb)

    level = jnp.log1p(demand_ref[...] + base_ref[...]).astype(bf16)
    feats = feat_ref[...].reshape((cin - 1) * slab_rows, width)
    ones = jnp.ones((slab_rows, width), bf16)
    x = jnp.concatenate([level, feats, ones], axis=0)
    cot = cot_ref[...]
    accb[0:slab_rows, :] += lanes(cot)
    b1 = col[0][:, 0:1]
    b2 = col[1][:, 0:1]
    ro = col[2][:, 0:1]
    for g in range(groups):
        r0 = g * rows_per
        cot_g = jnp.concatenate(
            [jnp.broadcast_to(cot[r0 + k : r0 + k + 1, :], (hidden, width)) for k in range(rows_per)], axis=0)
        v1 = jnp.dot(w1x[g], x, preferred_element_type=f32) + b1
        a1, s1 = gelu_both(v1)
        a1 = a1.astype(bf16)
        v2 = jnp.dot(w2x[...], a1, preferred_element_type=f32) + b2
        a2, s2 = gelu_both(v2)
        a2 = a2.astype(bf16)
        pred_ref[r0 : r0 + rows_per, :] = jnp.dot(rox[...], a2, preferred_element_type=f32)[0:rows_per] + rb_ref[0, 0]
        accr[...] += lanes(a2.astype(f32) * cot_g)
        d2f = (ro * cot_g) * s2
        acc_d2 = lanes(d2f)
        d2 = d2f.astype(bf16)
        accb[slab_rows : slab_rows + block, :] += acc_d2
        acc2[...] += lax.dot_general(d2, a1, NT, preferred_element_type=f32)
        back = jnp.dot(w2t[...], d2, preferred_element_type=f32)
        d1 = (back * s1).astype(bf16)
        acc1[g] += lax.dot_general(d1, x, NT, preferred_element_type=f32)

    @pl.when(step == pl.num_programs(0) - 1)
    def _():
        def fold(a):
            return sum(a[k * hidden : (k + 1) * hidden] for k in range(rows_per))

        total2 = acc2[...]
        g2 = sum(total2[k * hidden : (k + 1) * hidden, k * hidden : (k + 1) * hidden] for k in range(rows_per))
        total1 = jnp.zeros((hidden, depth), f32)
        for g in range(groups):
            keep = (iota((block, depth), 0) // hidden + g * rows_per) == iota((block, depth), 1) % slab_rows
            total1 += fold(jnp.where(keep, acc1[g], 0.0))
        gather = (iota((depth, hidden), 0) // slab_rows == iota((depth, hidden), 1)).astype(f32)
        g1 = jnp.dot(total1, gather, precision=lax.Precision.HIGHEST, preferred_element_type=f32)
        gr = fold(jnp.sum(accr[...], axis=1, keepdims=True))
        gb2 = fold(jnp.sum(accb[slab_rows : slab_rows + block, :], axis=1, keepdims=True))
        gb3 = jnp.sum(accb[0:slab_rows, :], keepdims=True)
        lane = iota((hidden, hidden), 1)
        right = jnp.where(lane == cin + 1, gr, jnp.where(lane == cin + 2, gb2, jnp.where(lane == cin + 3, gb3, g1)))
        packed = jnp.concatenate([g2, right], axis=1)
        n, k, _ = grads_ref.shape
        for j in range(n):
            grads_ref[j] = packed[j * k : (j + 1) * k]


def lanes(a):
    return sum(a[:, k * 128 : (k + 1) * 128] for k in range(a.shape[1] // 128))


def gelu_both(v):
    w = v * root_half
    phi = 0.5 + 0.5 * lax.erf(w)
    bell = jnp.exp2((w * w) * (-log2e))
    return v * phi, phi + (v * inv_root_tau) * bell


def mlp(demand, base, feats, cot, w1, b1, w2, b2, ro, rb, devices, rows_per=4, width=1024):
    slab_rows, w = demand.shape
    hidden, cin = w1.shape
    block = rows_per * hidden
    depth = (cin + 1) * slab_rows
    whole = lambda s: pl.BlockSpec(s, lambda i: tuple(0 for _ in s))
    cols = pl.BlockSpec((slab_rows, width), lambda i: (0, i))
    return pl.pallas_call(
        functools.partial(mlp_body, rows_per),
        grid=(w // width,),
        in_specs=[
            cols, pl.BlockSpec((1, width), lambda i: (0, i)),
            pl.BlockSpec((cin - 1, slab_rows, width), lambda i: (0, 0, i)), cols,
            whole((hidden, cin)), whole((1, hidden)), whole((hidden, hidden)), whole((1, hidden)), whole((1, hidden)),
            pl.BlockSpec(memory_space=pltpu.SMEM),
        ],
        out_specs=[cols, whole((devices, hidden // devices, 2 * hidden))],
        out_shape=[
            jax.ShapeDtypeStruct((slab_rows, w), f32),
            jax.ShapeDtypeStruct((devices, hidden // devices, 2 * hidden), f32),
        ],
        scratch_shapes=[
            pltpu.VMEM((slab_rows // rows_per, block, depth), bf16),
            pltpu.VMEM((block, block), bf16),
            pltpu.VMEM((block, block), bf16),
            pltpu.VMEM((8, block), bf16),
            pltpu.VMEM((3, block, 128), f32),
            pltpu.VMEM((slab_rows // rows_per, block, depth), f32),
            pltpu.VMEM((block, block), f32),
            pltpu.VMEM((block, 128), f32),
            pltpu.VMEM((slab_rows + block, 128), f32),
        ],
        name="mlp",
    )(demand, base, feats, cot, w1, b1[None, :], w2, b2[None, :], ro[None, :], rb[None, :])


def greet(n):
    me, group = lax.axis_index("canvas"), lax.axis_index("groups")
    barrier = pltpu.get_barrier_semaphore()

    def hail(k, carry):
        pl.semaphore_signal(
            barrier, inc=1, device_id=(group, lax.rem(me + k, n)), device_id_type=pl.DeviceIdType.MESH)
        return carry

    lax.fori_loop(1, n, hail, 0)
    pl.semaphore_wait(barrier, n - 1)


def swap(n, source, target, send_sem, recv_sem):
    me, group = lax.axis_index("canvas"), lax.axis_index("groups")

    def copy(k, slot):
        peer = lax.rem(me + k, n)
        return pltpu.make_async_remote_copy(
            src_ref=source.at[peer], dst_ref=target.at[slot], send_sem=send_sem.at[k], recv_sem=recv_sem.at[k],
            device_id=(group, peer), device_id_type=pl.DeviceIdType.MESH)

    def start(k, carry):
        copy(k, me).start()
        return carry

    def arrive(k, carry):
        copy(k, lax.rem(me + n - k, n)).wait_recv()
        return carry

    lax.fori_loop(1, n, start, 0)
    target[pl.ds(me, 1)] = source[pl.ds(me, 1)]
    lax.fori_loop(1, n, arrive, 0)

    def finish():
        def left(k, carry):
            copy(k, me).wait_send()
            return carry

        lax.fori_loop(1, n, left, 0)

    return finish


def items_body(n, send_ref, got_ref, send_sem, recv_sem):
    greet(n)
    swap(n, send_ref, got_ref, send_sem, recv_sem)()


def base_body(n, totals_ref, base_ref, got, result, back, send_a, recv_a, send_b, recv_b):
    greet(n)
    end_a = swap(n, totals_ref, got, send_a, recv_a)
    running = jnp.zeros(got.shape[1:], f32)
    for d in range(n):
        result[d] = running
        running = running + got[d]
    end_b = swap(n, result, back, send_b, recv_b)
    part = got.shape[2]
    for d in range(n):
        base_ref[:, d * part : (d + 1) * part] = back[d]
    end_a()
    end_b()


def sum_body(n, grads_ref, out_ref, got, result, back, send_a, recv_a, send_b, recv_b):
    greet(n)
    end_a = swap(n, grads_ref, got, send_a, recv_a)
    total = got[0]
    for d in range(1, n):
        total = total + got[d]
    for d in range(n):
        result[d] = total
    end_b = swap(n, result, back, send_b, recv_b)
    k = got.shape[1]
    for d in range(n):
        out_ref[d * k : (d + 1) * k, :] = back[d]
    end_a()
    end_b()


def linked(body, n, x, out_shape, phases, collective_id, name):
    vmem = pl.BlockSpec(memory_space=pltpu.VMEM)
    extra = [pltpu.VMEM(x.shape, f32)] * 3 if phases == 2 else []
    return pl.pallas_call(
        functools.partial(body, n),
        out_shape=jax.ShapeDtypeStruct(out_shape, f32),
        in_specs=[vmem],
        out_specs=vmem,
        scratch_shapes=extra + [pltpu.SemaphoreType.DMA((n,))] * (2 * phases),
        compiler_params=pltpu.CompilerParams(collective_id=collective_id, has_side_effects=True),
        name=name,
    )(x)


def slab_body(lane_group, got_ref, local_ref, totals_ref, acc):
    n, _, cap = got_ref.shape
    slab_rows, w = local_ref.shape
    tail = 128
    per = max(1, min(n, 2048 // cap))
    for c in range(n // per):
        def line(which):
            return jnp.concatenate([got_ref[c * per + j, which : which + 1, :] for j in range(per)], axis=1)

        value = line(0)
        place = line(1).astype(i32)
        end = line(2).astype(i32)
        row = place // w
        start = place - row * w
        group = start // lane_group
        first = start - group * lane_group
        last = end - group * lane_group
        key = group * slab_rows + row
        limit = (group + 1) * slab_rows
        hi = value.astype(bf16).astype(f32)
        lo = value - hi
        count = per * cap
        m = iota((acc.shape[0], count), 0)
        hot = jnp.where((m >= key) & (m < limit), 1.0, 0.0).astype(bf16)
        lane = iota((lane_group, count), 0)
        inside = (lane >= first) & (lane < last)
        over = (iota((tail, count), 0) + lane_group) < last
        fine = jnp.concatenate(
            [jnp.where(inside, hi, 0.0).astype(bf16), jnp.where(inside, lo, 0.0).astype(bf16),
             jnp.where(over, hi, 0.0).astype(bf16), jnp.where(over, lo, 0.0).astype(bf16)], axis=0)
        update = lax.dot_general(hot, fine, NT, preferred_element_type=f32)
        if c == 0:
            acc[...] = update
        else:
            acc[...] += update
    g2 = 2 * lane_group
    for q in range(w // lane_group):
        rows = slice(q * slab_rows, (q + 1) * slab_rows)
        main = acc[rows, 0:lane_group] + acc[rows, lane_group:g2]
        local_ref[:, q * lane_group : (q + 1) * lane_group] = main
        if q > 0:
            before = slice((q - 1) * slab_rows, q * slab_rows)
            spill = acc[before, g2 : g2 + tail] + acc[before, g2 + tail : g2 + 2 * tail]
            local_ref[:, q * lane_group : q * lane_group + tail] = main[:, 0:tail] + spill
    part = w // n
    for d in range(n):
        totals_ref[d] = local_ref[slab_rows - 1 : slab_rows, d * part : (d + 1) * part]


def slab(got, slab_rows, w, lane_group=256):
    n = got.shape[0]
    return pl.pallas_call(
        functools.partial(slab_body, lane_group),
        out_shape=[jax.ShapeDtypeStruct((slab_rows, w), f32), jax.ShapeDtypeStruct((n, 1, w // n), f32)],
        in_specs=[pl.BlockSpec(memory_space=pltpu.VMEM)],
        out_specs=[pl.BlockSpec(memory_space=pltpu.VMEM)] * 2,
        scratch_shapes=[pltpu.VMEM((slab_rows * w // lane_group, 2 * lane_group + 256), f32)],
        name="slab",
    )(got)


def per_device(
    net_slabs,
    row_offsets,
    left_column,
    column_span,
    pin_counts,
    tile_features,
    cotangent,
    first_weight,
    first_bias,
    second_weight,
    second_bias,
    readout_weight,
    readout_bias,
):
    devices = lax.axis_size("canvas")
    slab_rows = tile_features.shape[1]
    canvas_width = tile_features.shape[2]
    nets_here = pin_counts.shape[0]
    capacity = 4 * nets_here // devices
    highest = lax.Precision.HIGHEST
    first_is_low = net_slabs[:, 0] <= net_slabs[:, 1]
    low_slab = jnp.minimum(net_slabs[:, 0], net_slabs[:, 1])
    high_slab = jnp.maximum(net_slabs[:, 0], net_slabs[:, 1])
    low_offset = jnp.where(first_is_low, row_offsets[:, 0], row_offsets[:, 1])
    high_offset = jnp.where(first_is_low, row_offsets[:, 1], row_offsets[:, 0])
    right_edge = jnp.minimum(left_column + column_span, canvas_width)
    span_columns = (right_edge - left_column).astype(jnp.float32)
    span_rows = ((high_slab - low_slab) * slab_rows + high_offset - low_offset).astype(jnp.float32)
    net_weight = (
        jnp.sqrt(pin_counts.astype(jnp.float32))
        * (span_columns + span_rows)
        / (span_columns * span_rows)
    )
    target_slab = jnp.concatenate([low_slab, high_slab])
    local_row = jnp.concatenate([low_offset, high_offset])
    start_column = jnp.concatenate([left_column, left_column])
    end_column = jnp.concatenate([right_edge, right_edge])
    amounts = jnp.concatenate([net_weight, -net_weight])
    item_count = target_slab.shape[0]
    slab_ids = jnp.arange(devices, dtype=jnp.int32)
    slab_hot = (target_slab[:, None] == slab_ids[None, :]).astype(jnp.bfloat16)
    block_len = 128
    block_count = item_count // block_len
    blocked_hot = slab_hot.reshape(block_count, block_len, devices)
    lower_ones = (jnp.arange(block_len)[:, None] >= jnp.arange(block_len)[None, :]).astype(
        jnp.bfloat16
    )
    inclusive = jnp.einsum(
        "ij,bjd->bid", lower_ones, blocked_hot, preferred_element_type=jnp.float32
    )
    block_totals = inclusive[:, -1, :]
    block_start = jnp.cumsum(block_totals, axis=0) - block_totals
    counted = (inclusive + block_start[:, None, :] - 1.0) * blocked_hot.astype(jnp.float32)
    slot_rank = jnp.sum(counted, axis=2).reshape(item_count).astype(jnp.int32)
    payload = jnp.stack(
        [
            amounts,
            (local_row * canvas_width + start_column).astype(jnp.float32),
            end_column.astype(jnp.float32),
        ]
    )
    dest_mask = (slab_ids[:, None] == target_slab[None, :]).astype(jnp.float32)
    left_side = (dest_mask[:, None, :] * payload[None, :, :]).reshape(3 * devices, item_count)
    rank_hot = (slot_rank[:, None] == jnp.arange(capacity, dtype=jnp.int32)[None, :]).astype(
        jnp.float32
    )
    send_items = jnp.dot(
        left_side, rank_hot, precision=highest, preferred_element_type=jnp.float32
    ).reshape(devices, 3, capacity)
    got_items = linked(items_body, devices, send_items, send_items.shape, 1, 0, "items")
    local, totals = slab(got_items, slab_rows, canvas_width)
    base = linked(base_body, devices, totals, (1, canvas_width), 2, 1, "base")
    prediction, grads = mlp(
        local, base, tile_features, cotangent, first_weight, first_bias, second_weight, second_bias,
        readout_weight, readout_bias, devices)
    hidden, cin = first_weight.shape
    summed = linked(sum_body, devices, grads, (hidden, 2 * hidden), 2, 2, "sum")
    right = summed[:, hidden:]
    return (prediction, right[:, :cin], right[:, cin], summed[:, :hidden], right[:, cin + 2], right[:, cin + 1],
            right[0:1, cin + 3])


def solution(mesh):
    in_specs = (
        P(("groups", "canvas"), None),
        P(("groups", "canvas"), None),
        P(("groups", "canvas")),
        P(("groups", "canvas")),
        P(("groups", "canvas")),
        P(None, ("groups", "canvas"), None),
        P(("groups", "canvas"), None),
        P(),
        P(),
        P(),
        P(),
        P(),
        P(),
    )
    out_specs = (
        P(("groups", "canvas"), None),
        P("groups", None),
        P("groups"),
        P("groups", None),
        P("groups"),
        P("groups"),
        P("groups"),
    )
    return jax.shard_map(
        per_device, mesh=mesh, in_specs=in_specs, out_specs=out_specs, check_vma=False
    )
```

time: 403 us -> 117 us (0.29)
  matrix products: 153 us -> 3.37 us
  Pallas kernels: 0 us -> 102 us
  blocking collectives: 94.2 us -> 0 us
  loops' own time: 44.8 us -> 0 us
  other arithmetic: 44.9 us -> 1.56 us
  local copies, waits for them, and re-layouts: 46.6 us -> 8.65 us
  waiting for transfers between devices: 11.8 us -> 0 us
  starting transfers between devices: 4.03 us -> 0 us
    dot_general x98 -> x0, matrix products: 149 us -> none  [the longest x16 44.7 us: cell_block(): jnp.dot(second_weight, act_one, preferred_element_type=jnp.float32)]
    pallas_call x0 -> x5, Pallas kernels: none -> 102 us  [the longest x1 53.6 us: mlp(): pl.pallas_call(functools.partial(mlp_body, rows_per), grid=(w // width,),...]
    psum x1 -> x0, blocking collectives: 62 us -> none  [per_device(): lax.psum((totals[0], totals[1], totals[2], totals[3], totals[4], totals[5...]
    another operation x1 -> x0, loops' own time: 44.8 us -> none  [per_device(): lax.scan(row_step, start, jnp.arange(slab_rows, dtype=jnp.int32))]
    all_to_all x2 -> x0, blocking collectives: 32.2 us -> none  [the longest x1 17.1 us: per_device(): lax.all_to_all(across, 'canvas', split_axis=1, concat_axis=0, tiled=True)]
    dynamic_update_slice x16 -> x0, local copies, waits for them, and re-layouts: 28.3 us -> none  [per_device(): lax.scan(row_step, start, jnp.arange(slab_rows, dtype=jnp.int32))]
    reduce_sum x16 -> x0, other arithmetic: 26.1 us -> none  [cell_block(): grad_readout_bias = jnp.sum(grad_row).reshape(1)]
    all_to_all x1 -> x0, waiting for transfers between devices: 11.8 us -> none  [per_device(): lax.all_to_all(columns_done, 'canvas', split_axis=0, concat_axis=1, tiled...]
  transfers between devices with their start and end apart: 1 -> 0, of which waited for: 1 -> 0; matrix products, arithmetic and copies ran while one was open for 1% -> 0% of each run, Pallas kernels for 0% -> 0%
where the time goes in v1:
time: 117 us
  Pallas kernels  102 us (87%)
  local copies, waits for them, and re-layouts  8.65 us (7%)
  matrix products  3.37 us (3%)
  other arithmetic  1.56 us (1%)
  between operations  1.5 us (1%)
    pallas_call x1, Pallas kernels, mlp(): pl.pallas_call(functools.partial(mlp_body, rows_per), grid=(w // width,),...  53.6 us
    pallas_call x3, Pallas kernels, linked(): pl.pallas_call(functools.partial(body, n), out_shape=jax.ShapeDtypeStruct...  36.9 us
    pallas_call x1, Pallas kernels, slab(): pl.pallas_call(functools.partial(slab_body, lane_group), out_shape=[jax.S...  11.3 us
    dot_general x1, matrix products, per_device(): jnp.dot(left_side, rank_hot, precision=highest, preferred_element_type=jn...  3.18 us
    unnamed x11, local copies, waits for them, and re-layouts  2.76 us

profile of v1, /device:TPU:0, one launch (start us, length us, event | category | flops | bytes accessed | tf_op | source)
XLA Modules:
  0.0 116.9 jit_solution(3803268144777362647)
XLA Ops:
  0.6 0.8 slice_select_fusion
  1.5 0.1 copy.49
  1.6 0.0 copy-start
  1.6 0.0 copy-start.1
  1.6 0.2 iota_compare_fusion.1
  1.8 0.0 copy-start.2
  1.8 0.6 copy.50
  2.4 0.2 fusion.9
  2.6 0.5 copy.51
  3.1 0.1 copy.52
  3.3 0.1 copy.53
  3.3 0.4 multiply_reduce_fusion
  3.8 0.1 copy.54
  3.8 0.0 copy-done
  3.8 0.0 copy-done.1
  3.9 0.0 copy-done.2
  4.0 0.0 copy-start.3
  4.0 3.2 %fusion.1 = f32[16,3,512]{2,0,1:T(8,128)S(1)} fusion(s32[4096]{0:T(1024)S(1)} %bitcast.47, f32[3,4096]{1,0:T(4,128)S(1)} %pad_maximum_fusion, f32[16,4096]{1,0:T(8,128)S(1)} %fusion.7), kind=kOutput, calls=%fused_computation.2 | convolution fusion | flops 1210253312 | bytes 425984 | tf_op jit(solution)/shard_map/dot_general | solution.py:383
  7.2 0.7 copy.55.send_ref
  8.0 10.9 %items.1.got_ref = f32[16,3,512]{2,1,0:T(4,128)} custom-call(f32[16,3,512]{2,1,0:T(4,128)} %copy.55.send_ref), custom_call_target="tpu_custom_call" | custom-call | tf_op jit(solution)/shard_map/items/pallas_call | solution.py:244
  18.8 11.3 %slab.1 = (f32[16,8192]{1,0:T(8,128)}, f32[16,1,512]{2,1,0:T(1,128)}) custom-call(f32[16,3,512]{2,1,0:T(4,128)} %items.1.got_ref), custom_call_target="tpu_custom_call" | custom-call | tf_op jit(solution)/shard_map/slab/pallas_call | solution.py:306
  30.1 15.0 %base.1.base_ref = f32[1,8192]{1,0:T(1,128)} custom-call(f32[16,1,512]{2,1,0:T(1,128)} %get-tuple-element.12.totals_ref), custom_call_target="tpu_custom_call" | custom-call | tf_op jit(solution)/shard_map/base/pallas_call | solution.py:244
  45.1 0.0 copy-done.3
  45.1 0.7 copy.56.w1_ref
  46.5 53.6 %mlp.1 = (f32[16,8192]{1,0:T(8,128)}, f32[16,4,128]{2,1,0:T(4,128)}) custom-call(f32[16,8192]{1,0:T(8,128)} %get-tuple-element.11.demand_ref, f32[1,8192]{1,0:T(1,128)} %base.1.base_ref, bf16[7,16,8192]{2,1,0:T(8,128)(2,1)} %feat_ref.1, f32[16,8192]{1,0:T(8,128)} %cot_ref.1, bf16[64,8]{1,0:T(8,128)(2,1)} %copy.56.w1_ref, f32[1,64]{1,0:T(1,128)} %bitcast.48, ...), custom_call_target="tpu_custom_call" | custom-call | tf_op jit(solution)/shard_map/mlp/pallas_call | solution.py:132
  100.1 11.0 %sum.1 = f32[64,128]{1,0:T(8,128)} custom-call(f32[16,4,128]{2,1,0:T(4,128)} %get-tuple-element.14.grads_ref), custom_call_target="tpu_custom_call" | custom-call | tf_op jit(solution)/shard_map/sum/pallas_call | solution.py:244
  111.1 0.8 slice.50
  111.9 0.7 copy.57
  112.6 1.6 %slice_reduce_fusion = (f32[64]{0:T(128)}, f32[64]{0:T(128)}, f32[64]{0:T(128)}) fusion(f32[64,128]{1,0:T(8,128)} %sum.1), kind=kLoop, calls=%fused_computation.15 | loop fusion | bytes 1536 | tf_op jit(solution)/shard_map/slice | solution.py:395
  114.2 1.3 %slice.55 = f32[1,1]{1,0:T(1,128)} slice(f32[64,128]{1,0:T(8,128)} %sum.1), slice={[0:1], [75:76]} | slice | bytes 8 | tf_op jit(solution)/shard_map/slice | solution.py:396
  115.5 1.4 %copy.60 = f32[64,64]{1,0:T(8,128)} copy(f32[64,64]{1,0:T(8,128)} %bitcast.33) | data formatting | bytes 32768
  (12 shorter events, 0.2 us)
Async XLA Ops:
  1.6 2.2 %copy-start = (s32[2048]{0:T(1024)S(1)}, s32[2048]{0:T(1024)}, u32[]{:S(2)}) copy-start(s32[2048]{0:T(1024)} %param.15) | copy-start | bytes 24580
  1.6 2.2 %copy-start.1 = (s32[2048]{0:T(1024)S(1)}, s32[2048]{0:T(1024)}, u32[]{:S(2)}) copy-start(s32[2048]{0:T(1024)} %param.16) | copy-start | bytes 24580
  1.8 2.1 %copy-start.2 = (s32[2048]{0:T(1024)S(1)}, s32[2048]{0:T(1024)}, u32[]{:S(2)}) copy-start(s32[2048]{0:T(1024)} %param.17) | copy-start | bytes 24580
  4.0 41.1 %copy-start.3 = (bf16[64,8]{0,1:T(8,128)(2,1)S(1)}, bf16[64,8]{0,1:T(8,128)(2,1)}, u32[]{:S(2)}) copy-start(bf16[64,8]{0,1:T(8,128)(2,1)} %param.20) | copy-start | bytes 3076

commit v2 on v1

--- a/solution.py
+++ b/solution.py
@@ -202,27 +202,45 @@
     return finish
 
 
-def items_body(n, send_ref, got_ref, send_sem, recv_sem):
+def route_body(n, lane_group, send_ref, local_ref, base_ref, items, acc, totals, got, result, back,
+               send_a, recv_a, send_b, recv_b, send_c, recv_c):
     greet(n)
-    swap(n, send_ref, got_ref, send_sem, recv_sem)()
-
-
-def base_body(n, totals_ref, base_ref, got, result, back, send_a, recv_a, send_b, recv_b):
-    greet(n)
-    end_a = swap(n, totals_ref, got, send_a, recv_a)
+    end_a = swap(n, send_ref, items, send_a, recv_a)
+    slab(lane_group, items, local_ref, totals, acc)
+    end_b = swap(n, totals, got, send_b, recv_b)
     running = jnp.zeros(got.shape[1:], f32)
     for d in range(n):
         result[d] = running
         running = running + got[d]
-    end_b = swap(n, result, back, send_b, recv_b)
+    end_c = swap(n, result, back, send_c, recv_c)
     part = got.shape[2]
     for d in range(n):
         base_ref[:, d * part : (d + 1) * part] = back[d]
     end_a()
     end_b()
-
-
-def sum_body(n, grads_ref, out_ref, got, result, back, send_a, recv_a, send_b, recv_b):
+    end_c()
+
+
+def route(send, slab_rows, w, lane_group=256):
+    n = send.shape[0]
+    vmem = pl.BlockSpec(memory_space=pltpu.VMEM)
+    part = pltpu.VMEM((n, 1, w // n), f32)
+    return pl.pallas_call(
+        functools.partial(route_body, n, lane_group),
+        out_shape=[jax.ShapeDtypeStruct((slab_rows, w), f32), jax.ShapeDtypeStruct((1, w), f32)],
+        in_specs=[vmem],
+        out_specs=[vmem] * 2,
+        scratch_shapes=[
+            pltpu.VMEM(send.shape, f32), pltpu.VMEM((slab_rows * w // lane_group, 2 * lane_group + 256), f32),
+            part, part, part, part,
+        ] + [pltpu.SemaphoreType.DMA((n,))] * 6,
+        compiler_params=pltpu.CompilerParams(collective_id=0, has_side_effects=True),
+        name="route",
+    )(send)
+
+
+def sum_body(n, grads_ref, g1_ref, gb1_ref, g2_ref, gb2_ref, gr_ref, gb_ref, got, result, back, total_ref,
+             send_a, recv_a, send_b, recv_b):
     greet(n)
     end_a = swap(n, grads_ref, got, send_a, recv_a)
     total = got[0]
@@ -233,26 +251,46 @@
     end_b = swap(n, result, back, send_b, recv_b)
     k = got.shape[1]
     for d in range(n):
-        out_ref[d * k : (d + 1) * k, :] = back[d]
+        total_ref[d * k : (d + 1) * k, :] = back[d]
+    hidden, cin = g1_ref.shape
+    g2_ref[...] = total_ref[:, 0:hidden]
+    right = total_ref[:, hidden:]
+    g1_ref[...] = right[:, 0:cin]
+    eye = iota((hidden, hidden), 0) == iota((hidden, hidden), 1)
+
+    def row(lane):
+        return jnp.sum(jnp.where(eye, right[:, lane : lane + 1], 0.0), axis=0, keepdims=True)
+
+    gb1_ref[...] = row(cin)
+    gr_ref[...] = row(cin + 1)
+    gb2_ref[...] = row(cin + 2)
+    gb_ref[...] = right[0:1, cin + 3 : cin + 4]
     end_a()
     end_b()
 
 
-def linked(body, n, x, out_shape, phases, collective_id, name):
+def sum_all(grads, cin):
+    n, k, _ = grads.shape
+    hidden = n * k
     vmem = pl.BlockSpec(memory_space=pltpu.VMEM)
-    extra = [pltpu.VMEM(x.shape, f32)] * 3 if phases == 2 else []
+    line = (1, hidden)
     return pl.pallas_call(
-        functools.partial(body, n),
-        out_shape=jax.ShapeDtypeStruct(out_shape, f32),
+        functools.partial(sum_body, n),
+        out_shape=[
+            jax.ShapeDtypeStruct(shape, f32)
+            for shape in ((hidden, cin), line, (hidden, hidden), line, line, (1, 1))
+        ],
         in_specs=[vmem],
-        out_specs=vmem,
-        scratch_shapes=extra + [pltpu.SemaphoreType.DMA((n,))] * (2 * phases),
-        compiler_params=pltpu.CompilerParams(collective_id=collective_id, has_side_effects=True),
-        name=name,
-    )(x)
-
-
-def slab_body(lane_group, got_ref, local_ref, totals_ref, acc):
+        out_specs=[vmem] * 6,
+        scratch_shapes=[pltpu.VMEM(grads.shape, f32)] * 3
+        + [pltpu.VMEM((hidden, 2 * hidden), f32)]
+        + [pltpu.SemaphoreType.DMA((n,))] * 4,
+        compiler_params=pltpu.CompilerParams(collective_id=1, has_side_effects=True),
+        name="sum_all",
+    )(grads)
+
+
+def slab(lane_group, got_ref, local_ref, totals_ref, acc):
     n, _, cap = got_ref.shape
     slab_rows, w = local_ref.shape
     tail = 128
@@ -301,18 +339,6 @@
         totals_ref[d] = local_ref[slab_rows - 1 : slab_rows, d * part : (d + 1) * part]
 
 
-def slab(got, slab_rows, w, lane_group=256):
-    n = got.shape[0]
-    return pl.pallas_call(
-        functools.partial(slab_body, lane_group),
-        out_shape=[jax.ShapeDtypeStruct((slab_rows, w), f32), jax.ShapeDtypeStruct((n, 1, w // n), f32)],
-        in_specs=[pl.BlockSpec(memory_space=pltpu.VMEM)],
-        out_specs=[pl.BlockSpec(memory_space=pltpu.VMEM)] * 2,
-        scratch_shapes=[pltpu.VMEM((slab_rows * w // lane_group, 2 * lane_group + 256), f32)],
-        name="slab",
-    )(got)
-
-
 def per_device(
     net_slabs,
     row_offsets,
@@ -333,7 +359,6 @@
     canvas_width = tile_features.shape[2]
     nets_here = pin_counts.shape[0]
     capacity = 4 * nets_here // devices
-    highest = lax.Precision.HIGHEST
     first_is_low = net_slabs[:, 0] <= net_slabs[:, 1]
     low_slab = jnp.minimum(net_slabs[:, 0], net_slabs[:, 1])
     high_slab = jnp.maximum(net_slabs[:, 0], net_slabs[:, 1])
@@ -368,32 +393,34 @@
     block_start = jnp.cumsum(block_totals, axis=0) - block_totals
     counted = (inclusive + block_start[:, None, :] - 1.0) * blocked_hot.astype(jnp.float32)
     slot_rank = jnp.sum(counted, axis=2).reshape(item_count).astype(jnp.int32)
-    payload = jnp.stack(
+    high_amounts = lax.reduce_precision(amounts, 8, 7)
+    fine = 64
+    terms = jnp.stack(
         [
-            amounts,
-            (local_row * canvas_width + start_column).astype(jnp.float32),
-            end_column.astype(jnp.float32),
+            high_amounts,
+            amounts - high_amounts,
+            local_row.astype(jnp.float32),
+            (start_column // fine).astype(jnp.float32),
+            (start_column % fine).astype(jnp.float32),
+            (end_column - start_column).astype(jnp.float32),
         ]
-    )
-    dest_mask = (slab_ids[:, None] == target_slab[None, :]).astype(jnp.float32)
-    left_side = (dest_mask[:, None, :] * payload[None, :, :]).reshape(3 * devices, item_count)
+    ).astype(jnp.bfloat16)
+    dest_mask = (slab_ids[:, None] == target_slab[None, :]).astype(jnp.bfloat16)
+    left_side = (terms[:, None, :] * dest_mask[None, :, :]).reshape(6 * devices, item_count)
     rank_hot = (slot_rank[:, None] == jnp.arange(capacity, dtype=jnp.int32)[None, :]).astype(
-        jnp.float32
-    )
-    send_items = jnp.dot(
-        left_side, rank_hot, precision=highest, preferred_element_type=jnp.float32
-    ).reshape(devices, 3, capacity)
-    got_items = linked(items_body, devices, send_items, send_items.shape, 1, 0, "items")
-    local, totals = slab(got_items, slab_rows, canvas_width)
-    base = linked(base_body, devices, totals, (1, canvas_width), 2, 1, "base")
+        jnp.bfloat16
+    )
+    placed = jnp.dot(left_side, rank_hot, preferred_element_type=jnp.float32).reshape(6, devices, capacity)
+    first = placed[3] * fine + placed[4]
+    send_items = jnp.stack(
+        [placed[0] + placed[1], placed[2] * canvas_width + first, first + placed[5]], axis=1
+    )
+    local, base = route(send_items, slab_rows, canvas_width)
     prediction, grads = mlp(
         local, base, tile_features, cotangent, first_weight, first_bias, second_weight, second_bias,
         readout_weight, readout_bias, devices)
-    hidden, cin = first_weight.shape
-    summed = linked(sum_body, devices, grads, (hidden, 2 * hidden), 2, 2, "sum")
-    right = summed[:, hidden:]
-    return (prediction, right[:, :cin], right[:, cin], summed[:, :hidden], right[:, cin + 2], right[:, cin + 1],
-            right[0:1, cin + 3])
+    g1, gb1, g2, gb2, gr, gb = sum_all(grads, first_weight.shape[1])
+    return (prediction, g1, gb1[0], g2, gb2[0], gr[0], gb[0])
 
 
 def solution(mesh):

time: 117 us -> 118 us (level)
  other arithmetic: 1.56 us -> 5.49 us
  Pallas kernels: 102 us -> 98.3 us
  between operations: 1.5 us -> 3.22 us
  matrix products: 3.37 us -> 1.76 us
    unnamed x11 -> x8, local copies, waits for them, and re-layouts: 2.76 us -> 6.93 us
    slice x3 -> x0, local copies, waits for them, and re-layouts: 3.71 us -> none  [the longest x1 1.62 us: per_device(): right[:, cin + 1]]
    pallas_call x4 -> x2, Pallas kernels: 48.2 us -> 44.7 us  [the longest x1 30.3 us: route(): pl.pallas_call(functools.partial(route_body, n, lane_group), out_shape=[j...]
    another operation x1 -> x4, other arithmetic: 0.05 us -> 2.47 us  [per_device(): jnp.stack([amounts, (local_row * canvas_width + start_column).astype(jnp....]
    dot_general x1, matrix products: 3.18 us -> 1.57 us  [per_device(): jnp.dot(left_side, rank_hot, preferred_element_type=jnp.float32)]
where the time goes in v2:
time: 118 us; the launch traced here: 117 us
  Pallas kernels  98.3 us (83%)
  local copies, waits for them, and re-layouts  8.62 us (7%)
  other arithmetic  5.49 us (5%)
  between operations  3.22 us (3%)
  matrix products  1.76 us (1%)
    pallas_call x1, Pallas kernels, mlp(): pl.pallas_call(functools.partial(mlp_body, rows_per), grid=(w // width,),...  53.6 us
    pallas_call x1, Pallas kernels, route(): pl.pallas_call(functools.partial(route_body, n, lane_group), out_shape=[j...  30.3 us
    pallas_call x1, Pallas kernels, sum_all(): pl.pallas_call(functools.partial(sum_body, n), out_shape=[jax.ShapeDtypeS...  14.5 us
    unnamed x8, local copies, waits for them, and re-layouts  6.93 us

profile of v2, /device:TPU:0, one launch (start us, length us, event | category | flops | bytes accessed | tf_op | source)
XLA Modules:
  0.0 117.4 jit_solution(14304431351254320291)
XLA Ops:
  0.6 0.8 slice_select_fusion.1
  1.5 0.7 fusion.14
  2.3 0.7 add_minimum_fusion
  3.0 0.9 fusion.10
  3.8 0.8 convert_convert_fusion
  4.7 0.1 stack.4
  4.9 0.1 broadcast_multiply_fusion
  5.0 0.1 copy.49
  5.1 0.2 iota_compare_fusion.2
  5.2 0.6 copy.50
  5.8 0.2 fusion.4
  6.0 0.5 copy.51
  6.6 0.1 copy.52
  6.7 0.1 copy.53
  6.8 0.4 multiply_reduce_fusion
  7.2 0.1 copy.54
  7.3 0.0 copy-start
  7.3 1.6 %fusion = f32[96,512]{1,0:T(8,128)S(1)} fusion(bf16[96,4096]{1,0:T(8,128)(2,1)S(1)} %bitcast.37, s32[4096]{0:T(1024)S(1)} %bitcast.53), kind=kOutput, calls=%fused_computation.1 | convolution fusion | flops 404750336 | bytes 999424 | tf_op jit(solution)/shard_map/dot_general | solution.py:413
  9.0 0.7 pad_maximum_fusion.send_ref
  9.7 30.3 %route.1 = (f32[16,8192]{1,0:T(8,128)}, f32[1,8192]{1,0:T(1,128)}) custom-call(f32[16,3,512]{2,1,0:T(4,128)} %pad_maximum_fusion.send_ref), custom_call_target="tpu_custom_call" | custom-call | tf_op jit(solution)/shard_map/route/pallas_call | solution.py:228
  40.0 0.0 copy-done
  40.0 0.7 copy.56.w1_ref
  41.4 53.6 %mlp.1 = (f32[16,8192]{1,0:T(8,128)}, f32[16,4,128]{2,1,0:T(4,128)}) custom-call(f32[16,8192]{1,0:T(8,128)} %get-tuple-element.17.demand_ref, f32[1,8192]{1,0:T(1,128)} %get-tuple-element.18.base_ref, bf16[7,16,8192]{2,1,0:T(8,128)(2,1)} %feat_ref.1, f32[16,8192]{1,0:T(8,128)} %cot_ref.1, bf16[64,8]{1,0:T(8,128)(2,1)} %copy.56.w1_ref, f32[1,64]{1,0:T(1,128)} %bitcast.54, ...), custom_call_target="tpu_custom_call" | custom-call | tf_op jit(solution)/shard_map/mlp/pallas_call | solution.py:132
  94.9 14.5 %sum_all.1 = (f32[64,8]{1,0:T(8,128)}, f32[1,64]{1,0:T(1,128)}, f32[64,64]{1,0:T(8,128)}, f32[1,64]{1,0:T(1,128)}, f32[1,64]{1,0:T(1,128)}, /*index=5*/f32[1,1]{1,0:T(1,128)}) custom-call(f32[16,4,128]{2,1,0:T(4,128)} %get-tuple-element.20.grads_ref), custom_call_target="tpu_custom_call" | custom-call | tf_op jit(solution)/shard_map/sum_all/pallas_call | solution.py:277
  109.4 1.4 %copy.57 = f32[64,8]{0,1:T(8,128)} copy(f32[64,8]{1,0:T(8,128)} %get-tuple-element.56) | data formatting | bytes 4096
  110.8 1.1 copy.64
  111.9 1.4 %copy.65 = f32[64,64]{1,0:T(8,128)} copy(f32[64,64]{1,0:T(8,128)} %get-tuple-element.87) | data formatting | bytes 32768
  113.3 1.2 %copy.66 = f32[64]{0:T(128)} copy(f32[64]{0:T(128)} %bitcast.58) | data formatting | bytes 512
  114.5 1.2 copy.67
  (12 shorter events, 0.2 us)
Async XLA Ops:
  7.3 32.7 %copy-start = (bf16[64,8]{0,1:T(8,128)(2,1)S(1)}, bf16[64,8]{0,1:T(8,128)(2,1)}, u32[]{:S(2)}) copy-start(bf16[64,8]{0,1:T(8,128)(2,1)} %param.20) | copy-start | bytes 3076

commit v3 on v1

--- a/solution.py
+++ b/solution.py
@@ -12,6 +12,7 @@
 f32 = jnp.float32
 bf16 = jnp.bfloat16
 i32 = jnp.int32
+NARROW = (False, False)
 NT = (((1,), (1,)), ((), ()))
 
 
@@ -42,16 +43,16 @@
         same = iota((block, block), 0) // hidden == iota((block, block), 1) // hidden
         down = jnp.dot(pick, w2_ref[...], preferred_element_type=f32).astype(bf16)
         full = lax.dot_general(down, pick, NT, preferred_element_type=f32)
-        w2x[...] = jnp.where(same, full, 0.0).astype(bf16)
+        w2x[...] = jnp.where(same, 0.5 * full, 0.0).astype(bf16)
         flip = lax.dot_general(pick, w2_ref[...], (((1,), (1,)), ((), ())), preferred_element_type=f32).astype(bf16)
         full_t = lax.dot_general(flip, pick, NT, preferred_element_type=f32)
-        w2t[...] = jnp.where(same, full_t, 0.0).astype(bf16)
+        w2t[...] = jnp.where(same, 0.5 * full_t, 0.0).astype(bf16)
         ro_wide = lax.dot_general(ro_ref[...], pick, NT, preferred_element_type=f32)
         ro_rows = jnp.broadcast_to(ro_wide, (8, block))
-        rox[...] = jnp.where(iota((8, block), 0) == iota((8, block), 1) // hidden, ro_rows, 0.0).astype(bf16)
+        rox[...] = jnp.where(iota((8, block), 0) == iota((8, block), 1) // hidden, 0.5 * ro_rows, 0.0).astype(bf16)
         col[0] = jnp.broadcast_to(jnp.sum(pick_f * b1_ref[...], axis=1, keepdims=True), (block, 128))
         col[1] = jnp.broadcast_to(jnp.sum(pick_f * b2_ref[...], axis=1, keepdims=True), (block, 128))
-        col[2] = jnp.broadcast_to(jnp.sum(pick_f * ro_ref[...].astype(f32), axis=1, keepdims=True), (block, 128))
+        col[2] = 0.5 * jnp.broadcast_to(jnp.sum(pick_f * ro_ref[...].astype(f32), axis=1, keepdims=True), (block, 128))
         acc1[...] = jnp.zeros_like(acc1)
         acc2[...] = jnp.zeros_like(acc2)
         accr[...] = jnp.zeros_like(accr)
@@ -71,10 +72,10 @@
         cot_g = jnp.concatenate(
             [jnp.broadcast_to(cot[r0 + k : r0 + k + 1, :], (hidden, width)) for k in range(rows_per)], axis=0)
         v1 = jnp.dot(w1x[g], x, preferred_element_type=f32) + b1
-        a1, s1 = gelu_both(v1)
+        a1, s1 = gelu_twice(v1, NARROW[0])
         a1 = a1.astype(bf16)
         v2 = jnp.dot(w2x[...], a1, preferred_element_type=f32) + b2
-        a2, s2 = gelu_both(v2)
+        a2, s2 = gelu_twice(v2, NARROW[1])
         a2 = a2.astype(bf16)
         pred_ref[r0 : r0 + rows_per, :] = jnp.dot(rox[...], a2, preferred_element_type=f32)[0:rows_per] + rb_ref[0, 0]
         accr[...] += lanes(a2.astype(f32) * cot_g)
@@ -93,14 +94,14 @@
             return sum(a[k * hidden : (k + 1) * hidden] for k in range(rows_per))
 
         total2 = acc2[...]
-        g2 = sum(total2[k * hidden : (k + 1) * hidden, k * hidden : (k + 1) * hidden] for k in range(rows_per))
+        g2 = 0.5 * sum(total2[k * hidden : (k + 1) * hidden, k * hidden : (k + 1) * hidden] for k in range(rows_per))
         total1 = jnp.zeros((hidden, depth), f32)
         for g in range(groups):
             keep = (iota((block, depth), 0) // hidden + g * rows_per) == iota((block, depth), 1) % slab_rows
             total1 += fold(jnp.where(keep, acc1[g], 0.0))
         gather = (iota((depth, hidden), 0) // slab_rows == iota((depth, hidden), 1)).astype(f32)
         g1 = jnp.dot(total1, gather, precision=lax.Precision.HIGHEST, preferred_element_type=f32)
-        gr = fold(jnp.sum(accr[...], axis=1, keepdims=True))
+        gr = 0.5 * fold(jnp.sum(accr[...], axis=1, keepdims=True))
         gb2 = fold(jnp.sum(accb[slab_rows : slab_rows + block, :], axis=1, keepdims=True))
         gb3 = jnp.sum(accb[0:slab_rows, :], keepdims=True)
         lane = iota((hidden, hidden), 1)
@@ -115,11 +116,17 @@
     return sum(a[:, k * 128 : (k + 1) * 128] for k in range(a.shape[1] // 128))
 
 
-def gelu_both(v):
+def gelu_twice(v, narrow):
     w = v * root_half
-    phi = 0.5 + 0.5 * lax.erf(w)
+    if narrow:
+        w = w.astype(bf16)
+        tail = (v * (2.0 * inv_root_tau)).astype(bf16)
+        bell = jnp.exp2((w * w) * bf16(-log2e))
+        both = 1.0 + lax.erf(w).astype(f32)
+        return v * both, both + (tail * bell).astype(f32)
+    both = 1.0 + lax.erf(w)
     bell = jnp.exp2((w * w) * (-log2e))
-    return v * phi, phi + (v * inv_root_tau) * bell
+    return v * both, both + (v * (2.0 * inv_root_tau)) * bell
 
 
 def mlp(demand, base, feats, cot, w1, b1, w2, b2, ro, rb, devices, rows_per=4, width=1024):
@@ -202,27 +209,44 @@
     return finish
 
 
-def items_body(n, send_ref, got_ref, send_sem, recv_sem):
+def route_body(n, lane_group, send_ref, local_ref, base_ref, items, acc, totals, got, result, back,
+               send_a, recv_a, send_b, recv_b, send_c, recv_c):
     greet(n)
-    swap(n, send_ref, got_ref, send_sem, recv_sem)()
-
-
-def base_body(n, totals_ref, base_ref, got, result, back, send_a, recv_a, send_b, recv_b):
-    greet(n)
-    end_a = swap(n, totals_ref, got, send_a, recv_a)
+    end_a = swap(n, send_ref, items, send_a, recv_a)
+    slab(lane_group, items, local_ref, totals, acc)
+    end_b = swap(n, totals, got, send_b, recv_b)
     running = jnp.zeros(got.shape[1:], f32)
     for d in range(n):
         result[d] = running
         running = running + got[d]
-    end_b = swap(n, result, back, send_b, recv_b)
+    end_c = swap(n, result, back, send_c, recv_c)
     part = got.shape[2]
     for d in range(n):
         base_ref[:, d * part : (d + 1) * part] = back[d]
     end_a()
     end_b()
-
-
-def sum_body(n, grads_ref, out_ref, got, result, back, send_a, recv_a, send_b, recv_b):
+    end_c()
+
+
+def route(send, slab_rows, w, lane_group=256):
+    n = send.shape[0]
+    vmem = pl.BlockSpec(memory_space=pltpu.VMEM)
+    part = pltpu.VMEM((n, 1, w // n), f32)
+    return pl.pallas_call(
+        functools.partial(route_body, n, lane_group),
+        out_shape=[jax.ShapeDtypeStruct((slab_rows, w), f32), jax.ShapeDtypeStruct((1, w), f32)],
+        in_specs=[vmem],
+        out_specs=[vmem] * 2,
+        scratch_shapes=[
+            pltpu.VMEM(send.shape, f32), pltpu.VMEM((slab_rows * w // lane_group, 2 * lane_group + 256), f32),
+            part, part, part, part,
+        ] + [pltpu.SemaphoreType.DMA((n,))] * 6,
+        compiler_params=pltpu.CompilerParams(collective_id=0, has_side_effects=True),
+        name="route",
+    )(send)
+
+
+def sum_body(n, grads_ref, total_ref, got, result, back, send_a, recv_a, send_b, recv_b):
     greet(n)
     end_a = swap(n, grads_ref, got, send_a, recv_a)
     total = got[0]
@@ -233,9 +257,50 @@
     end_b = swap(n, result, back, send_b, recv_b)
     k = got.shape[1]
     for d in range(n):
-        out_ref[d * k : (d + 1) * k, :] = back[d]
+        total_ref[d * k : (d + 1) * k, :] = back[d]
     end_a()
     end_b()
+
+
+def split_body(total_ref, g1_out, gb1_out, g2_out, gb2_out, gr_out, gb_out,
+               g1_ref, gb1_ref, g2_ref, gb2_ref, gr_ref, gb_ref, out_sem):
+    cin, hidden = g1_ref.shape
+    g2_ref[...] = total_ref[:, 0:hidden]
+    right = total_ref[:, hidden:]
+    eye = iota((hidden, hidden), 0) == iota((hidden, hidden), 1)
+
+    def row(lane):
+        return jnp.sum(jnp.where(eye, right[:, lane : lane + 1], 0.0), axis=0, keepdims=True)
+
+    g1_ref[...] = jnp.concatenate([row(c) for c in range(cin)], axis=0)
+    gb1_ref[...] = row(cin).reshape(hidden)
+    gr_ref[...] = row(cin + 1).reshape(hidden)
+    gb2_ref[...] = row(cin + 2).reshape(hidden)
+    gb_ref[...] = right[0:1, cin + 3 : cin + 4].reshape(1)
+    pairs = ((g1_ref, g1_out), (gb1_ref, gb1_out), (g2_ref, g2_out), (gb2_ref, gb2_out), (gr_ref, gr_out),
+             (gb_ref, gb_out))
+    copies = [pltpu.make_async_copy(source, target, out_sem.at[i]) for i, (source, target) in enumerate(pairs)]
+    for c in copies:
+        c.start()
+    for c in copies:
+        c.wait()
+
+
+def sum_all(grads, cin):
+    n, k, _ = grads.shape
+    hidden = n * k
+    vmem = pl.BlockSpec(memory_space=pltpu.VMEM)
+    line = (hidden,)
+    shapes = ((cin, hidden), line, (hidden, hidden), line, line, (1,))
+    total = linked(sum_body, n, grads, (hidden, 2 * hidden), 2, 1, "sum_all")
+    return pl.pallas_call(
+        split_body,
+        out_shape=[jax.ShapeDtypeStruct(shape, f32) for shape in shapes],
+        in_specs=[vmem],
+        out_specs=[pl.BlockSpec(memory_space=pltpu.HBM)] * 6,
+        scratch_shapes=[pltpu.VMEM(shape, f32) for shape in shapes] + [pltpu.SemaphoreType.DMA((6,))],
+        name="split",
+    )(total)
 
 
 def linked(body, n, x, out_shape, phases, collective_id, name):
@@ -252,7 +317,7 @@
     )(x)
 
 
-def slab_body(lane_group, got_ref, local_ref, totals_ref, acc):
+def slab(lane_group, got_ref, local_ref, totals_ref, acc):
     n, _, cap = got_ref.shape
     slab_rows, w = local_ref.shape
     tail = 128
@@ -301,18 +366,6 @@
         totals_ref[d] = local_ref[slab_rows - 1 : slab_rows, d * part : (d + 1) * part]
 
 
-def slab(got, slab_rows, w, lane_group=256):
-    n = got.shape[0]
-    return pl.pallas_call(
-        functools.partial(slab_body, lane_group),
-        out_shape=[jax.ShapeDtypeStruct((slab_rows, w), f32), jax.ShapeDtypeStruct((n, 1, w // n), f32)],
-        in_specs=[pl.BlockSpec(memory_space=pltpu.VMEM)],
-        out_specs=[pl.BlockSpec(memory_space=pltpu.VMEM)] * 2,
-        scratch_shapes=[pltpu.VMEM((slab_rows * w // lane_group, 2 * lane_group + 256), f32)],
-        name="slab",
-    )(got)
-
-
 def per_device(
     net_slabs,
     row_offsets,
@@ -333,7 +386,6 @@
     canvas_width = tile_features.shape[2]
     nets_here = pin_counts.shape[0]
     capacity = 4 * nets_here // devices
-    highest = lax.Precision.HIGHEST
     first_is_low = net_slabs[:, 0] <= net_slabs[:, 1]
     low_slab = jnp.minimum(net_slabs[:, 0], net_slabs[:, 1])
     high_slab = jnp.maximum(net_slabs[:, 0], net_slabs[:, 1])
@@ -353,6 +405,7 @@
     end_column = jnp.concatenate([right_edge, right_edge])
     amounts = jnp.concatenate([net_weight, -net_weight])
     item_count = target_slab.shape[0]
+    highest = lax.Precision.HIGHEST
     slab_ids = jnp.arange(devices, dtype=jnp.int32)
     slab_hot = (target_slab[:, None] == slab_ids[None, :]).astype(jnp.bfloat16)
     block_len = 128
@@ -383,17 +436,12 @@
     send_items = jnp.dot(
         left_side, rank_hot, precision=highest, preferred_element_type=jnp.float32
     ).reshape(devices, 3, capacity)
-    got_items = linked(items_body, devices, send_items, send_items.shape, 1, 0, "items")
-    local, totals = slab(got_items, slab_rows, canvas_width)
-    base = linked(base_body, devices, totals, (1, canvas_width), 2, 1, "base")
+    local, base = route(send_items, slab_rows, canvas_width)
     prediction, grads = mlp(
         local, base, tile_features, cotangent, first_weight, first_bias, second_weight, second_bias,
         readout_weight, readout_bias, devices)
-    hidden, cin = first_weight.shape
-    summed = linked(sum_body, devices, grads, (hidden, 2 * hidden), 2, 2, "sum")
-    right = summed[:, hidden:]
-    return (prediction, right[:, :cin], right[:, cin], summed[:, :hidden], right[:, cin + 2], right[:, cin + 1],
-            right[0:1, cin + 3])
+    g1, gb1, g2, gb2, gr, gb = sum_all(grads, first_weight.shape[1])
+    return (prediction, g1.T, gb1, g2, gb2, gr, gb)
 
 
 def solution(mesh):

time: 117 us -> 110 us (0.940)
  local copies, waits for them, and re-layouts: 8.65 us -> 2.89 us
  Pallas kernels: 102 us -> 99.7 us
    pallas_call x3 -> x1, Pallas kernels: 36.9 us -> 14.3 us  [linked(): pl.pallas_call(functools.partial(body, n), out_shape=jax.ShapeDtypeStruct...]
    pallas_call x1 -> x2, Pallas kernels: 11.3 us -> 31.9 us  [the longest x1 30.3 us: route(): pl.pallas_call(functools.partial(route_body, n, lane_group), out_shape=[j...]
    slice x3 -> x0, local copies, waits for them, and re-layouts: 3.71 us -> none  [the longest x1 1.62 us: per_device(): right[:, cin + 1]]
    unnamed x11 -> x9, local copies, waits for them, and re-layouts: 2.76 us -> 0.71 us
where the time goes in v3:
time: 110 us; the launch traced here: 109 us
  Pallas kernels  99.7 us (91%)
  matrix products  3.37 us (3%)
  local copies, waits for them, and re-layouts  2.89 us (3%)
  between operations  1.67 us (2%)
  other arithmetic  1.56 us (1%)
    pallas_call x1, Pallas kernels, mlp(): pl.pallas_call(functools.partial(mlp_body, rows_per), grid=(w // width,),...  53.5 us
    pallas_call x1, Pallas kernels, route(): pl.pallas_call(functools.partial(route_body, n, lane_group), out_shape=[j...  30.3 us
    pallas_call x1, Pallas kernels, linked(): pl.pallas_call(functools.partial(body, n), out_shape=jax.ShapeDtypeStruct...  14.3 us
    dot_general x1, matrix products, per_device(): jnp.dot(left_side, rank_hot, precision=highest, preferred_element_type=jn...  3.18 us

profile of v3, /device:TPU:0, one launch (start us, length us, event | category | flops | bytes accessed | tf_op | source)
XLA Modules:
  0.0 109.2 jit_solution(355473776727241395)
XLA Ops:
  0.6 0.8 slice_select_fusion
  1.5 0.1 copy.45
  1.6 0.0 copy-start
  1.6 0.0 copy-start.1
  1.6 0.2 iota_compare_fusion.1
  1.8 0.0 copy-start.2
  1.8 0.6 copy.46
  2.4 0.2 fusion.9
  2.6 0.5 copy.47
  3.1 0.1 copy.48
  3.3 0.1 copy.49
  3.3 0.4 multiply_reduce_fusion
  3.8 0.1 copy.50
  3.8 0.0 copy-done
  3.8 0.0 copy-done.1
  3.9 0.0 copy-done.2
  4.0 0.0 copy-start.3
  4.0 3.2 %fusion.1 = f32[16,3,512]{2,0,1:T(8,128)S(1)} fusion(s32[4096]{0:T(1024)S(1)} %bitcast.45, f32[3,4096]{1,0:T(4,128)S(1)} %pad_maximum_fusion, f32[16,4096]{1,0:T(8,128)S(1)} %fusion.7), kind=kOutput, calls=%fused_computation.2 | convolution fusion | flops 1210253312 | bytes 425984 | tf_op jit(solution)/shard_map/dot_general | solution.py:436
  7.2 0.7 copy.51.send_ref
  8.0 30.3 %route.1 = (f32[16,8192]{1,0:T(8,128)}, f32[1,8192]{1,0:T(1,128)}) custom-call(f32[16,3,512]{2,1,0:T(4,128)} %copy.51.send_ref), custom_call_target="tpu_custom_call" | custom-call | tf_op jit(solution)/shard_map/route/pallas_call | solution.py:235
  38.2 0.0 copy-done.3
  38.3 0.7 copy.52.w1_ref
  39.6 53.5 %mlp.1 = (f32[16,8192]{1,0:T(8,128)}, f32[16,4,128]{2,1,0:T(4,128)}) custom-call(f32[16,8192]{1,0:T(8,128)} %get-tuple-element.17.demand_ref, f32[1,8192]{1,0:T(1,128)} %get-tuple-element.18.base_ref, bf16[7,16,8192]{2,1,0:T(8,128)(2,1)} %feat_ref.1, f32[16,8192]{1,0:T(8,128)} %cot_ref.1, bf16[64,8]{1,0:T(8,128)(2,1)} %copy.52.w1_ref, f32[1,64]{1,0:T(1,128)} %bitcast.46, ...), custom_call_target="tpu_custom_call" | custom-call | tf_op jit(solution)/shard_map/mlp/pallas_call | solution.py:139
  93.1 14.3 %sum_all.1.total_ref = f32[64,128]{1,0:T(8,128)} custom-call(f32[16,4,128]{2,1,0:T(4,128)} %get-tuple-element.20.grads_ref), custom_call_target="tpu_custom_call" | custom-call | tf_op jit(solution)/shard_map/sum_all/pallas_call | solution.py:309
  107.4 1.6 %split.1 = (f32[8,64]{1,0:T(8,128)}, f32[64]{0:T(128)}, f32[64,64]{1,0:T(8,128)}, f32[64]{0:T(128)}, f32[64]{0:T(128)}, /*index=5*/f32[1]{0:T(128)}) custom-call(f32[64,128]{1,0:T(8,128)} %sum_all.1.total_ref), custom_call_target="tpu_custom_call" | custom-call | tf_op jit(solution)/shard_map/split/pallas_call | solution.py:296
  (12 shorter events, 0.2 us)
Async XLA Ops:
  1.6 2.2 %copy-start = (s32[2048]{0:T(1024)S(1)}, s32[2048]{0:T(1024)}, u32[]{:S(2)}) copy-start(s32[2048]{0:T(1024)} %param.15) | copy-start | bytes 24580
  1.6 2.2 %copy-start.1 = (s32[2048]{0:T(1024)S(1)}, s32[2048]{0:T(1024)}, u32[]{:S(2)}) copy-start(s32[2048]{0:T(1024)} %param.16) | copy-start | bytes 24580
  1.8 2.1 %copy-start.2 = (s32[2048]{0:T(1024)S(1)}, s32[2048]{0:T(1024)}, u32[]{:S(2)}) copy-start(s32[2048]{0:T(1024)} %param.17) | copy-start | bytes 24580
  4.0 34.3 %copy-start.3 = (bf16[64,8]{0,1:T(8,128)(2,1)S(1)}, bf16[64,8]{0,1:T(8,128)(2,1)}, u32[]{:S(2)}) copy-start(bf16[64,8]{0,1:T(8,128)(2,1)} %param.20) | copy-start | bytes 3076
